TPU v7x, 256 devices: a whole 4x4x8 slice. The times are simulated.
256 devices in a mesh: seq: 16 (over z, core), pipe: 4 (over y), dp: 4 (over x).
Axes of the slice: x: 4, y: 4, z: 8, core: 2. Of those that a mesh axis runs over, the one named last changes fastest.
Arguments:
- segment_input: bfloat16 [4, 4096, 3072], P('pipe', ('dp', 'seq')), parts along dimension 1
- output_grad: bfloat16 [4, 4096, 3072], P('pipe', ('dp', 'seq')), parts along dimension 1, may hold values from -6 to 6
- qkv_weight: bfloat16 [4, 3072, 16, 384], P('pipe', None, 'seq')
- out_weight: bfloat16 [4, 2048, 3072], P('pipe', 'seq'), may hold values from -0.125 to 0.125
- query_gain: float32 [4, 128], P('pipe')
- key_gain: float32 [4, 128], P('pipe')
- gate_scale: float32 [4, 3072], P('pipe'), may hold values from -4 to 4
- neighbours: int32 [64, 27], P('dp'), parts along dimension 0, may hold values from -1 to 15
- tile_slot: int32 [64], P('dp'), parts along dimension 0, may hold values from 0 to 15, as said below
Outputs:
- segment_output: bfloat16 [4, 4096, 3072], P('pipe', ('dp', 'seq')), parts along dimension 1
- input_grad: bfloat16 [4, 4096, 3072], P('pipe', ('dp', 'seq')), parts along dimension 1
- gate_grad: float32 [16, 3072], P(('dp', 'pipe'), 'seq'), parts along dimension 0
There are 4 independent parts, one for each index of `dp`. A program takes and returns all parts, laid end to end along the dimension named above; an argument that names none is the same for every part. Nothing has to cross between parts.
Inputs may be any that keep to these rules, and one draw needn't show every extreme that they name: `tile_slot`: A permutation of 0 to 15.
All inputs are finite; a program needn't handle non-finite values.
Results may differ from a plain program's by a relative error of at most 0.02.
Values may be sent and summed in bfloat16 or wider, within the bound.
A program may use at most 128 MiB of HBM per device.

v0:
```python
import math
import jax
import jax.numpy as jnp
from jax import lax
from jax.sharding import PartitionSpec as P

TILE = 64
EPSILON = 1e-06


def passed_along(block, axis, distance):
    devices = range(lax.axis_size(axis))
    route = [((i - distance) % len(devices), i) for i in devices]
    return lax.ppermute(block, axis, route)


def slot_lists(neighbours, tile_slot):
    tile_count = tile_slot.shape[0]
    numbering = jnp.arange(tile_count, dtype=jnp.int32)
    placed = (tile_slot[:, None] == numbering[None, :]).astype(jnp.int32)
    tile_of_slot = jnp.sum(placed * numbering[:, None], axis=0)
    chosen = (tile_of_slot[:, None] == numbering[None, :]).astype(jnp.int32)
    listed_tiles = jnp.sum(chosen[:, :, None] * neighbours[None, :, :], axis=1)
    key_valid = listed_tiles >= 0
    safe_tiles = jnp.maximum(listed_tiles, 0)
    matches = (safe_tiles[:, :, None] == numbering[None, None, :]).astype(jnp.int32)
    key_slots = jnp.sum(matches * tile_slot[None, None, :], axis=2)
    return (key_slots, key_valid)


def block_tiles(tile_count):
    return math.gcd(tile_count, max(1, 512 // TILE))


def unit_norm(values):
    spread = jnp.sqrt(jnp.mean(values * values, axis=-1, keepdims=True) + EPSILON)
    return (values / spread, spread)


def probabilities(query_block, key_rows, block_valid):
    scores = jnp.einsum(
        "aihd,ajhd->ahij", query_block, key_rows, preferred_element_type=jnp.float32
    ) * (1.0 / math.sqrt(query_block.shape[-1]))
    key_mask = jnp.repeat(block_valid, TILE, axis=1)
    scores = jnp.where(key_mask[:, None, None, :], scores, -jnp.inf)
    row_max = jnp.max(scores, axis=-1, keepdims=True)
    weights = jnp.exp(scores - row_max)
    return (weights / jnp.sum(weights, axis=-1, keepdims=True)).astype(jnp.bfloat16)


def gathered(tiles_array, block_slots):
    picked = tiles_array[block_slots]
    return picked.reshape(block_slots.shape[0], -1, tiles_array.shape[2], tiles_array.shape[3])


def attend_both(query_tiles, key_tiles, value_tiles, grad_tiles, key_slots, key_valid):
    tile_count = query_tiles.shape[0]
    span = block_tiles(tile_count)
    scale_factor = 1.0 / math.sqrt(query_tiles.shape[-1])
    empty_grad = jnp.zeros(query_tiles.shape, jnp.float32)

    def per_block(accumulators, block_index):
        key_total, value_total = accumulators
        first_tile = block_index * span
        query_block = lax.dynamic_slice_in_dim(query_tiles, first_tile, span, 0)
        grad_block = lax.dynamic_slice_in_dim(grad_tiles, first_tile, span, 0)
        block_slots = lax.dynamic_slice_in_dim(key_slots, first_tile, span, 0)
        block_valid = lax.dynamic_slice_in_dim(key_valid, first_tile, span, 0)
        key_rows = gathered(key_tiles, block_slots)
        value_rows = gathered(value_tiles, block_slots)
        weights = probabilities(query_block, key_rows, block_valid)
        attended = jnp.einsum(
            "ahij,ajhd->aihd", weights, value_rows, preferred_element_type=jnp.float32
        )
        value_part = jnp.einsum(
            "ahij,aihd->ajhd", weights, grad_block, preferred_element_type=jnp.float32
        )
        prob_grad = jnp.einsum(
            "aihd,ajhd->ahij", grad_block, value_rows, preferred_element_type=jnp.float32
        )
        weights_wide = weights.astype(jnp.float32)
        row_delta = jnp.sum(weights_wide * prob_grad, axis=-1, keepdims=True)
        score_grad = (weights_wide * (prob_grad - row_delta) * scale_factor).astype(jnp.bfloat16)
        query_part = jnp.einsum(
            "ahij,ajhd->aihd", score_grad, key_rows, preferred_element_type=jnp.float32
        )
        key_part = jnp.einsum(
            "ahij,aihd->ajhd", score_grad, query_block, preferred_element_type=jnp.float32
        )
        block_shape = (span, block_slots.shape[1]) + query_tiles.shape[1:]
        key_total = key_total.at[block_slots].add(key_part.reshape(block_shape))
        value_total = value_total.at[block_slots].add(value_part.reshape(block_shape))
        return ((key_total, value_total), (attended, query_part))

    totals, parts = lax.scan(
        per_block, (empty_grad, empty_grad), jnp.arange(tile_count // span, dtype=jnp.int32)
    )
    flat_shape = (-1,) + query_tiles.shape[2:]
    return (
        parts[0].reshape(flat_shape),
        parts[1].reshape(flat_shape),
        totals[0].reshape(flat_shape),
        totals[1].reshape(flat_shape),
    )


def body(
    segment_input,
    output_grad,
    qkv_weight,
    out_weight,
    query_gain,
    key_gain,
    gate_scale,
    neighbours,
    tile_slot,
):
    key_slots, key_valid = slot_lists(neighbours, tile_slot)
    stream = segment_input[0]
    upstream = output_grad[0]
    model_width = stream.shape[1]
    head_dim = query_gain.shape[1]
    local_heads = qkv_weight.shape[2]
    local_width = local_heads * head_dim
    proj_weight = qkv_weight[0].reshape(model_width, local_heads * 3 * head_dim)
    out_local = out_weight[0]
    gate_row = gate_scale[0]
    query_weights = query_gain[0]
    key_weights = key_gain[0]
    projected = jnp.dot(
        lax.all_gather(stream, "seq", axis=0, tiled=True),
        proj_weight,
        preferred_element_type=jnp.float32,
    )
    all_tokens = projected.shape[0]
    projected = projected.reshape(all_tokens, local_heads, 3, head_dim)
    query_unit, query_spread = unit_norm(projected[:, :, 0])
    key_unit, key_spread = unit_norm(projected[:, :, 1])
    queries = (query_unit * query_weights).astype(jnp.bfloat16)
    keys_normed = (key_unit * key_weights).astype(jnp.bfloat16)
    value_rows = projected[:, :, 2].astype(jnp.bfloat16)
    scaled = (upstream.astype(jnp.float32) * gate_row).astype(jnp.bfloat16)
    attended_grad = jnp.einsum(
        "td,cd->tc",
        lax.all_gather(scaled, "seq", axis=0, tiled=True),
        out_local,
        preferred_element_type=jnp.float32,
    ).astype(jnp.bfloat16)

    def as_tiles(values):
        return values.reshape(-1, TILE, local_heads, head_dim)

    attended, query_grad, key_grad, value_grad = attend_both(
        as_tiles(queries),
        as_tiles(keys_normed),
        as_tiles(value_rows),
        as_tiles(attended_grad),
        key_slots,
        key_valid,
    )
    attended_low = attended.astype(jnp.bfloat16).reshape(all_tokens, local_width)
    rows = attended_low
    attention_out = lax.psum_scatter(
        jnp.dot(rows, out_local, preferred_element_type=jnp.float32),
        "seq",
        scatter_dimension=0,
        tiled=True,
    )
    section_out = (stream.astype(jnp.float32) + gate_row * attention_out).astype(jnp.bfloat16)
    segment_output = passed_along(section_out, "pipe", 1)
    gate_local = lax.psum_scatter(
        jnp.sum(upstream.astype(jnp.float32) * attention_out, axis=0),
        "seq",
        scatter_dimension=0,
        tiled=True,
    )
    query_scaled = query_grad * query_weights
    query_part_grad = (
        query_scaled - query_unit * jnp.mean(query_scaled * query_unit, axis=-1, keepdims=True)
    ) / query_spread
    key_scaled = key_grad * key_weights
    key_part_grad = (
        key_scaled - key_unit * jnp.mean(key_scaled * key_unit, axis=-1, keepdims=True)
    ) / key_spread
    projected_grad = (
        jnp.stack([query_part_grad, key_part_grad, value_grad], axis=2)
        .astype(jnp.bfloat16)
        .reshape(all_tokens, local_heads * 3 * head_dim)
    )
    rows = projected_grad
    stream_grad = lax.psum_scatter(
        jnp.einsum("tc,dc->td", rows, proj_weight, preferred_element_type=jnp.float32).astype(
            jnp.bfloat16
        ),
        "seq",
        scatter_dimension=0,
        tiled=True,
    ).astype(jnp.float32)
    token_grad = (upstream.astype(jnp.float32) + stream_grad).astype(jnp.bfloat16)
    input_grad = passed_along(token_grad, "pipe", -1)
    return (segment_output[None], input_grad[None], gate_local[None])


def solution(mesh):
    in_specs = (
        P("pipe", ("dp", "seq"), None),
        P("pipe", ("dp", "seq"), None),
        P("pipe", None, "seq", None),
        P("pipe", "seq", None),
        P("pipe", None),
        P("pipe", None),
        P("pipe", None),
        P("dp", None),
        P("dp"),
    )
    out_specs = (
        P("pipe", ("dp", "seq"), None),
        P("pipe", ("dp", "seq"), None),
        P(("dp", "pipe"), "seq"),
    )
    return jax.shard_map(body, mesh=mesh, in_specs=in_specs, out_specs=out_specs, check_vma=False)
```

profile of v0, /device:TPU:2, one launch (start us, length us, event | category | flops | bytes accessed | tf_op | source)
XLA Modules:
  0.0 510.5 jit_solution(14000528992266416604)
XLA Ops:
  13.2 45.7 %all-gather.6.cloned.1.call-done = bf16[1,1024,3072]{2,1,0:T(8,128)(2,1)} async-done(((bf16[1,64,3072]{2,1,0:T(8,128)(2,1)}), bf16[1,1024,3072]{2,1,0:T(8,128)(2,1)}) %all-gather.6.cloned.1.call-update) | async-done | bytes 6291472 | tf_op jit(solution)/shard_map/all_gather | solution.py:131
  58.9 5.5 %fusion.43 = f32[1024,1,3,128]{3,0,2,1:T(8,128)S(1)} fusion(bf16[3,128,3072]{2,1,0:T(8,128)(2,1)S(1)} %bitcast.180, bf16[1,1024,3072]{2,1,0:T(8,128)(2,1)} %all-gather.6.cloned.1.call-done), kind=kOutput, calls=%fused_computation.52 | convolution fusion | flops 2415919104 | bytes 10223616 | tf_op jit(solution)/shard_map/dot_general | solution.py:130
  67.4 38.6 %all-gather.4.cloned.1.call-done = bf16[1024,3072]{1,0:T(8,128)(2,1)} async-done(((bf16[64,3072]{1,0:T(8,128)(2,1)}), bf16[1024,3072]{1,0:T(8,128)(2,1)}) %all-gather.4.cloned.1.call-update) | async-done | bytes 6291472 | tf_op jit(solution)/shard_map/all_gather | solution.py:145
  106.0 4.6 convolution_convert_fusion.1
  110.8 179.4 %while.16 = (s32[]{:T(128)}, f32[16,64,1,128]{3,1,0,2:T(8,128)S(1)}, f32[16,64,1,128]{3,1,0,2:T(8,128)S(1)}, bf16[2,8,64,1,128]{4,2,1,3,0:T(8,128)(2,1)}, f32[2,...) while((s32[]{:T(128)}, ...), condition=%wide.region_11.12_spmd, body=%wide.region_5.11_spmd.sunk | while | flops 1380196096 | bytes 147397712 | solution.py:95
  118.4 5.3 %exponential_reduce_fusion.2 = (f32[8,64]{1,0:T(8,128)S(1)}, f32[8,64,1728]{2,1,0:T(8,128)}) fusion(bf16[8,1728,128]{2,1,0:T(8,128)(2,1)} %bitcast.173, pred[8,1728]{1,0:T(8,128)(4,1)S(1)} %broadcast_in_dim.84, bf16[16,64,1,128]{3,1,0,2:T(8,128)(2,1)S(1)} %get-tuple-element.237, s32[]{:T(128)S(6)} %select_n.30), kind=kOutput, calls=%fused_computation.13.clone.1 | convolution fusion | flops 230033088 | bytes 7225348 | tf_op jit(solution)/shard_map/while/body/eval_jaxpr/sub | solution.py:47
  129.3 3.2 fusion.94
  132.5 7.1 %fusion.98 = f32[2,8,64,1,128]{4,2,1,3,0:T(8,128)} fusion(f32[2,8,64,1,128]{4,2,1,3,0:T(8,128)} %get-tuple-element.218, s32[]{:T(128)S(6)} %copy.34, bf16[8,1728,128]{2,1,0:T(8,128)(2,1)} %bitcast.174, bf16[8,64,1728]{2,1,0:T(8,128)(2,1)} %copy-done.2, f32[8,64,1728]{2,1,0:T(8,128)} %fusion.94), kind=kOutput, calls=%fused_computation.20.clone.1 | convolution fusion | flops 232687808 | bytes 14811140 | tf_op jit(solution)/shard_map/while/body/eval_jaxpr/ahij,ajhd->aihd/dot_general | solution.py:84
  139.6 8.8 %fusion.95 = f32[8,128,1728]{1,2,0:T(8,128)} fusion(bf16[8,64,1728]{2,1,0:T(8,128)(2,1)} %copy-done.2, f32[8,64,1728]{2,1,0:T(8,128)} %fusion.94, bf16[16,64,1,128]{3,1,0,2:T(8,128)(2,1)S(1)} %get-tuple-element.237, s32[]{:T(128)S(6)} %select_n.30), kind=kOutput, calls=%fused_computation.16.clone.1 | convolution fusion | flops 232687808 | bytes 18219012 | tf_op jit(solution)/shard_map/while/body/eval_jaxpr/ahij,aihd->ajhd/dot_general | solution.py:87
  148.4 23.2 %scatter_fusion = f32[16,64,128]{2,1,0:T(8,128)S(1)} fusion(f32[16,64,128]{2,1,0:T(8,128)S(1)} %bitcast.162, s32[216]{0:T(256)S(1)} %reshape.617, f32[216,64,128]{2,1,0:T(8,128)} %bitcast.172), kind=kCustom, calls=%fused_computation.2.clone.1 | custom fusion | flops 1769472 | bytes 21234528 | tf_op jit(solution)/shard_map/while/body/eval_jaxpr/scatter-add | solution.py:91
  171.6 5.7 %fusion.96 = f32[8,128,1728]{1,2,0:T(8,128)} fusion(bf16[8,64,1728]{2,1,0:T(8,128)(2,1)} %copy-done.2, bf16[16,64,1,128]{3,1,0,2:T(8,128)(2,1)S(1)} %get-tuple-element.240, s32[]{:T(128)S(6)} %select_n.30), kind=kOutput, calls=%fused_computation.23.clone.1 | convolution fusion | flops 226492416 | bytes 8978436 | tf_op jit(solution)/shard_map/while/body/eval_jaxpr/ahij,aihd->ajhd/dot_general | solution.py:75
  177.3 23.2 %scatter_fusion.1 = f32[16,64,128]{2,1,0:T(8,128)S(1)} fusion(f32[16,64,128]{2,1,0:T(8,128)S(1)} %bitcast.164, s32[216]{0:T(256)S(1)} %reshape.617, f32[216,64,128]{2,1,0:T(8,128)} %bitcast.171), kind=kCustom, calls=%fused_computation.3.clone.1 | custom fusion | flops 1769472 | bytes 21234528 | tf_op jit(solution)/shard_map/while/body/eval_jaxpr/scatter-add | solution.py:92
  208.0 5.3 %exponential_reduce_fusion.2 = (f32[8,64]{1,0:T(8,128)S(1)}, f32[8,64,1728]{2,1,0:T(8,128)}) fusion(bf16[8,1728,128]{2,1,0:T(8,128)(2,1)} %bitcast.173, pred[8,1728]{1,0:T(8,128)(4,1)S(1)} %broadcast_in_dim.84, bf16[16,64,1,128]{3,1,0,2:T(8,128)(2,1)S(1)} %get-tuple-element.237, s32[]{:T(128)S(6)} %select_n.30), kind=kOutput, calls=%fused_computation.13.clone.1 | convolution fusion | flops 230033088 | bytes 7225348 | tf_op jit(solution)/shard_map/while/body/eval_jaxpr/sub | solution.py:47
  218.9 3.2 fusion.94
  222.1 7.1 %fusion.98 = f32[2,8,64,1,128]{4,2,1,3,0:T(8,128)} fusion(f32[2,8,64,1,128]{4,2,1,3,0:T(8,128)} %get-tuple-element.218, s32[]{:T(128)S(6)} %copy.34, bf16[8,1728,128]{2,1,0:T(8,128)(2,1)} %bitcast.174, bf16[8,64,1728]{2,1,0:T(8,128)(2,1)} %copy-done.2, f32[8,64,1728]{2,1,0:T(8,128)} %fusion.94), kind=kOutput, calls=%fused_computation.20.clone.1 | convolution fusion | flops 232687808 | bytes 14811140 | tf_op jit(solution)/shard_map/while/body/eval_jaxpr/ahij,ajhd->aihd/dot_general | solution.py:84
  229.2 8.8 %fusion.95 = f32[8,128,1728]{1,2,0:T(8,128)} fusion(bf16[8,64,1728]{2,1,0:T(8,128)(2,1)} %copy-done.2, f32[8,64,1728]{2,1,0:T(8,128)} %fusion.94, bf16[16,64,1,128]{3,1,0,2:T(8,128)(2,1)S(1)} %get-tuple-element.237, s32[]{:T(128)S(6)} %select_n.30), kind=kOutput, calls=%fused_computation.16.clone.1 | convolution fusion | flops 232687808 | bytes 18219012 | tf_op jit(solution)/shard_map/while/body/eval_jaxpr/ahij,aihd->ajhd/dot_general | solution.py:87
  238.0 23.2 %scatter_fusion = f32[16,64,128]{2,1,0:T(8,128)S(1)} fusion(f32[16,64,128]{2,1,0:T(8,128)S(1)} %bitcast.162, s32[216]{0:T(256)S(1)} %reshape.617, f32[216,64,128]{2,1,0:T(8,128)} %bitcast.172), kind=kCustom, calls=%fused_computation.2.clone.1 | custom fusion | flops 1769472 | bytes 21234528 | tf_op jit(solution)/shard_map/while/body/eval_jaxpr/scatter-add | solution.py:91
  261.2 5.7 %fusion.96 = f32[8,128,1728]{1,2,0:T(8,128)} fusion(bf16[8,64,1728]{2,1,0:T(8,128)(2,1)} %copy-done.2, bf16[16,64,1,128]{3,1,0,2:T(8,128)(2,1)S(1)} %get-tuple-element.240, s32[]{:T(128)S(6)} %select_n.30), kind=kOutput, calls=%fused_computation.23.clone.1 | convolution fusion | flops 226492416 | bytes 8978436 | tf_op jit(solution)/shard_map/while/body/eval_jaxpr/ahij,aihd->ajhd/dot_general | solution.py:75
  266.9 23.2 %scatter_fusion.1 = f32[16,64,128]{2,1,0:T(8,128)S(1)} fusion(f32[16,64,128]{2,1,0:T(8,128)S(1)} %bitcast.164, s32[216]{0:T(256)S(1)} %reshape.617, f32[216,64,128]{2,1,0:T(8,128)} %bitcast.171), kind=kCustom, calls=%fused_computation.3.clone.1 | custom fusion | flops 1769472 | bytes 21234528 | tf_op jit(solution)/shard_map/while/body/eval_jaxpr/scatter-add | solution.py:92
  295.9 7.1 %convolution_convert_fusion = bf16[1024,3072]{1,0:T(8,128)(2,1)} fusion(bf16[1024,384]{0,1:T(8,128)(2,1)S(1)} %bitcast.183, bf16[1,3072,1,384]{3,1,2,0:T(8,128)(2,1)} %param.13), kind=kOutput, calls=%fused_computation.50 | convolution fusion | flops 2419064832 | bytes 9437184 | tf_op jit(solution)/shard_map/tc,dc->td/dot_general | solution.py:192
  303.9 6.4 %fusion.50 = f32[1024,3072]{1,0:T(8,128)} fusion(bf16[1024,128]{1,0:T(8,128)(2,1)S(1)} %bitcast.186, bf16[1,128,3072]{2,1,0:T(8,128)(2,1)S(1)} %copy-done), kind=kOutput, calls=%fused_computation.63 | convolution fusion | flops 805306368 | bytes 13631488 | tf_op jit(solution)/shard_map/dot_general | solution.py:164
  310.3 58.0 %reduce-scatter.5.cloned.1.call-done = bf16[64,3072]{1,0:T(8,128)(2,1)} async-done(((bf16[1024,3072]{1,0:T(8,128)(2,1)}), bf16[64,3072]{1,0:T(8,128)(2,1)}) %reduce-scatter.5.cloned.1.call-update) | async-done | bytes 393232 | tf_op jit(solution)/shard_map/reduce_scatter | solution.py:191
  368.3 80.7 %reduce-scatter.3.cloned.1.call-done = f32[64,3072]{1,0:T(8,128)} async-done(((f32[1024,3072]{1,0:T(8,128)}), f32[64,3072]{1,0:T(8,128)}) %reduce-scatter.3.cloned.1.call-update) | async-done | bytes 786448 | tf_op jit(solution)/shard_map/reduce_scatter | solution.py:163
  455.1 46.7 %all-reduce = f32[3072]{0:T(1024)S(1)} all-reduce(f32[3072]{0:T(1024)S(1)} %get-tuple-element.116), channel_id=5, replica_groups=mesh['seq'=16,'pipe'=4,'dp'=4] {'seq'}, use_global_device_ids=true, to_apply=%region_17.18.clone | all-reduce | flops 3072 | bytes 24576
  (132 shorter events, 47.6 us)
Async XLA Ops:
  7.2 98.8 %copy-start = (bf16[1,128,3072]{2,1,0:T(8,128)(2,1)S(1)}, bf16[1,128,3072]{2,1,0:T(8,128)(2,1)}, u32[]{:S(2)}) copy-start(bf16[1,128,3072]{2,1,0:T(8,128)(2,1)} %param.14) | copy-start | bytes 2359300
  7.2 51.7 %all-gather.6.cloned.1.call-start = ((), (), s32[]{:S(2)}) async-start(), calls=%async_computation.5 | async-start | bytes 6684672 | tf_op jit(solution)/shard_map/all_gather | solution.py:131
  7.9 98.1 %all-gather.4.cloned.1.call-start = ((), (), s32[]{:S(2)}) async-start(), calls=%async_computation.2 | async-start | bytes 6684672 | tf_op jit(solution)/shard_map/all_gather | solution.py:145
  9.8 358.5 %reduce-scatter.5.cloned.1.call-start = ((), (), s32[]{:S(2)}) async-start(), calls=%async_computation.4 | async-start | bytes 6684672 | tf_op jit(solution)/shard_map/reduce_scatter | solution.py:191
  58.9 8.1 %copy-start.21 = (f32[1,128]{1,0:T(1,128)S(1)}, f32[1,128]{1,0:T(1,128)}, u32[]{:S(2)}) copy-start(f32[1,128]{1,0:T(1,128)} %param.15) | copy-start | bytes 1540
  58.9 8.3 %copy-start.23 = (f32[1,128]{1,0:T(1,128)S(1)}, f32[1,128]{1,0:T(1,128)}, u32[]{:S(2)}) copy-start(f32[1,128]{1,0:T(1,128)} %param.16) | copy-start | bytes 1540
  65.9 44.6 %copy-start.3 = (f32[1024,1,1,128]{3,0,2,1:T(8,128)}, f32[1024,1,1,128]{3,0,2,1:T(8,128)S(1)}, u32[]{:S(2)}) copy-start(f32[1024,1,1,128]{3,0,2,1:T(8,128)S(1)} %get-tuple-element.115) | copy-start | bytes 1572868
  66.0 44.6 %copy-start.5 = (f32[1024,1,1,128]{3,0,2,1:T(8,128)}, f32[1024,1,1,128]{3,0,2,1:T(8,128)S(1)}, u32[]{:S(2)}) copy-start(f32[1024,1,1,128]{3,0,2,1:T(8,128)S(1)} %get-tuple-element.114) | copy-start | bytes 1572868
  66.0 44.6 %copy-start.17 = (f32[1024]{0:T(1024)}, f32[1024]{0:T(1024)S(1)}, u32[]{:S(2)}) copy-start(f32[1024]{0:T(1024)S(1)} %get-tuple-element.119) | copy-start | bytes 12292
  67.0 43.6 %copy-start.12 = (f32[16,64]{1,0:T(8,128)}, f32[16,64]{1,0:T(8,128)S(1)}, u32[]{:S(2)}) copy-start(f32[16,64]{1,0:T(8,128)S(1)} %sqrt.31) | copy-start | bytes 12292
  110.7 179.4 %copy-start.13 = (f32[16,64]{1,0:T(8,128)S(1)}, f32[16,64]{1,0:T(8,128)}, u32[]{:S(2)}) copy-start(f32[16,64]{1,0:T(8,128)} %copy-done.12) | copy-start | bytes 12292
  110.7 179.4 %copy-start.24 = (f32[1,128]{1,0:T(1,128)S(1)}, f32[1,128]{1,0:T(1,128)}, u32[]{:S(2)}) copy-start(f32[1,128]{1,0:T(1,128)} %param.16) | copy-start | bytes 1540
  110.7 180.9 %copy-start.4 = (f32[1024,1,1,128]{3,0,2,1:T(8,128)S(1)}, f32[1024,1,1,128]{3,0,2,1:T(8,128)}, u32[]{:S(2)}) copy-start(f32[1024,1,1,128]{3,0,2,1:T(8,128)} %copy-done.3) | copy-start | bytes 1572868
  110.8 180.9 %copy-start.19 = (f32[2,8,64]{2,1,0:T(8,128)S(1)}, f32[2,8,64]{2,1,0:T(8,128)}, u32[]{:S(2)}) copy-start(f32[2,8,64]{2,1,0:T(8,128)} %sqrt.32) | copy-start | bytes 12292
  110.8 180.9 %copy-start.22 = (f32[1,128]{1,0:T(1,128)S(1)}, f32[1,128]{1,0:T(1,128)}, u32[]{:S(2)}) copy-start(f32[1,128]{1,0:T(1,128)} %param.15) | copy-start | bytes 1540
  110.8 182.5 %copy-start.15 = (f32[1024]{0:T(1024)S(1)}, f32[1024]{0:T(1024)}, u32[]{:S(2)}) copy-start(f32[1024]{0:T(1024)} %copy-done.14) | copy-start | bytes 12292
  110.8 182.5 %copy-start.18 = (f32[1024]{0:T(1024)S(1)}, f32[1024]{0:T(1024)}, u32[]{:S(2)}) copy-start(f32[1024]{0:T(1024)} %copy-done.17) | copy-start | bytes 12292
  303.0 146.0 %reduce-scatter.3.cloned.1.call-start = ((), (), s32[]{:S(2)}) async-start(), calls=%async_computation.3 | async-start | bytes 13369344 | tf_op jit(solution)/shard_map/reduce_scatter | solution.py:163
  310.3 138.8 %copy-start.7 = (bf16[1,64,3072]{2,1,0:T(8,128)(2,1)S(1)}, bf16[1,64,3072]{2,1,0:T(8,128)(2,1)}, u32[]{:S(2)}) copy-start(bf16[1,64,3072]{2,1,0:T(8,128)(2,1)} %param.11) | copy-start | bytes 1179652
  310.3 138.8 %copy-start.8 = (bf16[1,64,3072]{2,1,0:T(8,128)(2,1)S(1)}, bf16[1,64,3072]{2,1,0:T(8,128)(2,1)}, u32[]{:S(2)}) copy-start(bf16[1,64,3072]{2,1,0:T(8,128)(2,1)} %param.12) | copy-start | bytes 1179652
  310.3 138.8 %copy-start.16 = (f32[1,3072]{1,0:T(1,128)S(1)}, f32[1,3072]{1,0:T(1,128)}, u32[]{:S(2)}) copy-start(f32[1,3072]{1,0:T(1,128)} %param.17) | copy-start | bytes 36868
  310.3 143.6 %copy-start.26 = (u32[256]{0:T(256)S(1)}, u32[256]{0:T(256)}, u32[]{:S(2)}) copy-start(u32[256]{0:T(256)} %constant.48) | copy-start | bytes 3076
  450.6 51.9 %collective-permute-start = (bf16[64,3072]{1,0:T(8,128)(2,1)S(1)}, bf16[64,3072]{1,0:T(8,128)(2,1)S(1)}, u32[]{:S(2)}, u32[]{:S(2)}) collective-permute-start(bf16[64,3072]{1,0:T(8,128)(2,1)S(1)} %get-tuple-element.117), channel_id=1, source_target_pairs={{12,0},{0,4},{4,8},{8,12},{13,1},{1,5},{5,9},{9,13},{14,2},{2,6},{... | collective-permute-start | bytes 1179656 | tf_op jit(solution)/shard_map/ppermute | solution.py:14
  452.1 50.3 %collective-permute-start.1 = (bf16[64,3072]{1,0:T(8,128)(2,1)S(1)}, bf16[64,3072]{1,0:T(8,128)(2,1)S(1)}, u32[]{:S(2)}, u32[]{:S(2)}) collective-permute-start(bf16[64,3072]{1,0:T(8,128)(2,1)S(1)} %get-tuple-element.118), channel_id=1, source_target_pairs={{4,0},{8,4},{12,8},{0,12},{5,1},{9,5},{13,9},{1,13},{6,2},{10,6},{... | collective-permute-start | bytes 1179656 | tf_op jit(solution)/shard_map/ppermute | solution.py:14
  (13 other events, 34.6 us)
Sparse Core Ops, SparseCore 0:
  9.9 48.9 all-gather.5
  61.3 44.6 all-gather.3
  303.1 65.1 reduce-scatter.4
  370.7 78.2 reduce-scatter.2
where the time goes:
time: 514 us; the launch traced here: 511 us
  waiting for transfers between devices  224 us (44%)
  other arithmetic  108 us (21%)
  matrix products  85.4 us (17%)
  blocking collectives  46.7 us (9%)
  local copies, waits for them, and re-layouts  26.4 us (5%)
  between operations  14.8 us (3%)
    reduce_scatter x1, waiting for transfers between devices, body(): lax.psum_scatter(jnp.dot(rows, out_local, preferred_element_type=jnp.floa...  80.7 us
    reduce_scatter x1, waiting for transfers between devices, body(): lax.psum_scatter(jnp.einsum('tc,dc->td', rows, proj_weight, preferred_ele...  58 us
    unnamed x1, blocking collectives  46.7 us
    scatter-add x2, other arithmetic, per_block(): key_total = key_total.at[block_slots].add(key_part.reshape(block_shape))  46.5 us
    scatter-add x2, other arithmetic, per_block(): value_total.at[block_slots].add(value_part.reshape(block_shape))  46.5 us
    all_gather x1, waiting for transfers between devices, body(): lax.all_gather(stream, 'seq', axis=0, tiled=True)  45.7 us
    all_gather x1, waiting for transfers between devices, body(): lax.all_gather(scaled, 'seq', axis=0, tiled=True)  38.6 us
    dot_general x2, matrix products, per_block(): jnp.einsum('ahij,aihd->ajhd', score_grad, query_block, preferred_element_...  17.5 us
  transfers between devices with their start and end apart: 6, of which 4 were waited for; matrix products, arithmetic and copies ran while one was open for 4% of the time, Pallas kernels for 0%

commit v1 on v0

--- a/solution.py
+++ b/solution.py
@@ -127,10 +127,17 @@
     gate_row = gate_scale[0]
     query_weights = query_gain[0]
     key_weights = key_gain[0]
+    _make_plane = lambda page, mesh_name, on_dim: jnp.concatenate(
+        jax.lax.all_to_all(
+            jnp.stack(jax.lax.axis_size(mesh_name) * [page], 0),
+            mesh_name,
+            split_axis=0,
+            concat_axis=0,
+        ),
+        on_dim,
+    )
     projected = jnp.dot(
-        lax.all_gather(stream, "seq", axis=0, tiled=True),
-        proj_weight,
-        preferred_element_type=jnp.float32,
+        _make_plane(stream, "seq", 0), proj_weight, preferred_element_type=jnp.float32
     )
     all_tokens = projected.shape[0]
     projected = projected.reshape(all_tokens, local_heads, 3, head_dim)

time: 514 us -> 607 us (1.18)
  waiting for transfers between devices: 224 us -> 302 us
  starting transfers between devices: 3.47 us -> 12.2 us
    all_to_all x0 -> x1, waiting for transfers between devices: none -> 163 us  [body(): jax.lax.all_to_all(jnp.stack(jax.lax.axis_size(mesh_name) * [page], 0), m...]
    all_gather x1 -> x0, waiting for transfers between devices: 45.7 us -> none  [body(): lax.all_gather(stream, 'seq', axis=0, tiled=True)]
    all_gather x1, waiting for transfers between devices: 38.6 us -> 0.02 us  [body(): lax.all_gather(scaled, 'seq', axis=0, tiled=True)]
    all_to_all x0 -> x1, starting transfers between devices: none -> 8.75 us  [body(): jax.lax.all_to_all(jnp.stack(jax.lax.axis_size(mesh_name) * [page], 0), m...]
  transfers between devices with their start and end apart: 6 -> 6, of which waited for: 4 -> 3; matrix products, arithmetic and copies ran while one was open for 4% -> 3% of each run, Pallas kernels for 0% -> 0%
where the time goes in v1:
time: 607 us; the launch traced here: 604 us
  waiting for transfers between devices  302 us (50%)
  other arithmetic  107 us (18%)
  matrix products  86.1 us (14%)
  blocking collectives  46.7 us (8%)
  local copies, waits for them, and re-layouts  32.3 us (5%)
  between operations  14.9 us (2%)
  starting transfers between devices  12.2 us (2%)
    all_to_all x1, waiting for transfers between devices, body(): jax.lax.all_to_all(jnp.stack(jax.lax.axis_size(mesh_name) * [page], 0), m...  163 us
    reduce_scatter x1, waiting for transfers between devices, body(): lax.psum_scatter(jnp.dot(rows, out_local, preferred_element_type=jnp.floa...  80.7 us
    reduce_scatter x1, waiting for transfers between devices, body(): lax.psum_scatter(jnp.einsum('tc,dc->td', rows, proj_weight, preferred_ele...  58.6 us
    unnamed x1, blocking collectives  46.7 us
    scatter-add x2, other arithmetic, per_block(): key_total = key_total.at[block_slots].add(key_part.reshape(block_shape))  46.5 us
    scatter-add x2, other arithmetic, per_block(): value_total.at[block_slots].add(value_part.reshape(block_shape))  46.5 us
    dot_general x2, matrix products, per_block(): jnp.einsum('ahij,aihd->ajhd', score_grad, query_block, preferred_element_...  17.5 us
    dot_general x2, matrix products, per_block(): jnp.einsum('ahij,ajhd->aihd', score_grad, key_rows, preferred_element_typ...  14.2 us
  transfers between devices with their start and end apart: 6, of which 3 were waited for; matrix products, arithmetic and copies ran while one was open for 3% of the time, Pallas kernels for 0%

profile of v1, /device:TPU:2, one launch (start us, length us, event | category | flops | bytes accessed | tf_op | source)
XLA Modules:
  0.0 603.5 jit_solution(16983403864259728617)
XLA Ops:
  7.2 4.5 stack.10
  11.7 8.7 %all-to-all-start = ((bf16[16,64,3072]{2,1,0:T(8,128)(2,1)}), bf16[16,64,3072]{2,1,0:T(8,128)(2,1)}, u32[]{:S(2)}, u32[]{:S(2)}) async-start(bf16[16,64,3072]{2,1,0:T(8,128)(2,1)} %stack.10), calls=%async_computation | async-start | bytes 12582912 | tf_op jit(solution)/shard_map/all_to_all | solution.py:131
  21.4 4.3 copy.22
  26.1 163.0 %all-to-all-done = bf16[16,64,3072]{2,1,0:T(8,128)(2,1)} async-done(((bf16[16,64,3072]{2,1,0:T(8,128)(2,1)}), bf16[16,64,3072]{2,1,0:T(8,128)(2,1)}, u32[]{:S(2)}, u32[]{:S(2)}) %all-to-all-start) | async-done | bytes 6291488 | tf_op jit(solution)/shard_map/all_to_all | solution.py:131
  189.1 6.3 %convolution_bitcast_fusion.1 = f32[1024,1,3,128]{3,0,2,1:T(8,128)S(1)} fusion(bf16[1024,3072,1]{1,0,2:T(8,128)(2,1)} %bitcast.26, bf16[3,128,3072]{2,1,0:T(8,128)(2,1)} %bitcast.177), kind=kOutput, calls=%fused_computation.50 | convolution fusion | flops 2415919104 | bytes 10223616 | tf_op jit(solution)/shard_map/dot_general | solution.py:139
  198.4 4.6 convolution_convert_fusion.1
  203.2 179.4 %while.16 = (s32[]{:T(128)}, f32[16,64,1,128]{3,1,0,2:T(8,128)S(1)}, f32[16,64,1,128]{3,1,0,2:T(8,128)S(1)}, bf16[2,8,64,1,128]{4,2,1,3,0:T(8,128)(2,1)}, f32[2,...) while((s32[]{:T(128)}, ...), condition=%wide.region_11.12_spmd, body=%wide.region_5.11_spmd.sunk | while | flops 1380196096 | bytes 147397712 | solution.py:95
  210.8 5.3 exponential_reduce_fusion.2
  224.9 7.1 %fusion.93 = f32[2,8,64,1,128]{4,2,1,3,0:T(8,128)} fusion(f32[2,8,64,1,128]{4,2,1,3,0:T(8,128)} %get-tuple-element.218, s32[]{:T(128)S(6)} %copy.34, bf16[8,1728,128]{2,1,0:T(8,128)(2,1)} %bitcast.171, bf16[8,64,1728]{2,1,0:T(8,128)(2,1)} %copy-done.2, f32[8,64,1728]{2,1,0:T(8,128)} %fusion.89), kind=kOutput, calls=%fused_computation.20.clone.1 | convolution fusion | flops 232687808 | bytes 14811140 | tf_op jit(solution)/shard_map/while/body/eval_jaxpr/ahij,ajhd->aihd/dot_general | solution.py:84
  232.0 8.8 %fusion.90 = f32[8,128,1728]{1,2,0:T(8,128)} fusion(bf16[8,64,1728]{2,1,0:T(8,128)(2,1)} %copy-done.2, f32[8,64,1728]{2,1,0:T(8,128)} %fusion.89, bf16[16,64,1,128]{3,1,0,2:T(8,128)(2,1)S(1)} %get-tuple-element.237, s32[]{:T(128)S(6)} %select_n.30), kind=kOutput, calls=%fused_computation.16.clone.1 | convolution fusion | flops 232687808 | bytes 18219012 | tf_op jit(solution)/shard_map/while/body/eval_jaxpr/ahij,aihd->ajhd/dot_general | solution.py:87
  240.8 23.2 %scatter_fusion = f32[16,64,128]{2,1,0:T(8,128)S(1)} fusion(f32[16,64,128]{2,1,0:T(8,128)S(1)} %bitcast.159, s32[216]{0:T(256)S(1)} %reshape.620, f32[216,64,128]{2,1,0:T(8,128)} %bitcast.169), kind=kCustom, calls=%fused_computation.2.clone.1 | custom fusion | flops 1769472 | bytes 21234528 | tf_op jit(solution)/shard_map/while/body/eval_jaxpr/scatter-add | solution.py:91
  264.1 5.7 fusion.91
  269.7 23.2 %scatter_fusion.1 = f32[16,64,128]{2,1,0:T(8,128)S(1)} fusion(f32[16,64,128]{2,1,0:T(8,128)S(1)} %bitcast.161, s32[216]{0:T(256)S(1)} %reshape.620, f32[216,64,128]{2,1,0:T(8,128)} %bitcast.168), kind=kCustom, calls=%fused_computation.3.clone.1 | custom fusion | flops 1769472 | bytes 21234528 | tf_op jit(solution)/shard_map/while/body/eval_jaxpr/scatter-add | solution.py:92
  300.4 5.3 exponential_reduce_fusion.2
  314.5 7.1 %fusion.93 = f32[2,8,64,1,128]{4,2,1,3,0:T(8,128)} fusion(f32[2,8,64,1,128]{4,2,1,3,0:T(8,128)} %get-tuple-element.218, s32[]{:T(128)S(6)} %copy.34, bf16[8,1728,128]{2,1,0:T(8,128)(2,1)} %bitcast.171, bf16[8,64,1728]{2,1,0:T(8,128)(2,1)} %copy-done.2, f32[8,64,1728]{2,1,0:T(8,128)} %fusion.89), kind=kOutput, calls=%fused_computation.20.clone.1 | convolution fusion | flops 232687808 | bytes 14811140 | tf_op jit(solution)/shard_map/while/body/eval_jaxpr/ahij,ajhd->aihd/dot_general | solution.py:84
  321.6 8.8 %fusion.90 = f32[8,128,1728]{1,2,0:T(8,128)} fusion(bf16[8,64,1728]{2,1,0:T(8,128)(2,1)} %copy-done.2, f32[8,64,1728]{2,1,0:T(8,128)} %fusion.89, bf16[16,64,1,128]{3,1,0,2:T(8,128)(2,1)S(1)} %get-tuple-element.237, s32[]{:T(128)S(6)} %select_n.30), kind=kOutput, calls=%fused_computation.16.clone.1 | convolution fusion | flops 232687808 | bytes 18219012 | tf_op jit(solution)/shard_map/while/body/eval_jaxpr/ahij,aihd->ajhd/dot_general | solution.py:87
  330.4 23.2 %scatter_fusion = f32[16,64,128]{2,1,0:T(8,128)S(1)} fusion(f32[16,64,128]{2,1,0:T(8,128)S(1)} %bitcast.159, s32[216]{0:T(256)S(1)} %reshape.620, f32[216,64,128]{2,1,0:T(8,128)} %bitcast.169), kind=kCustom, calls=%fused_computation.2.clone.1 | custom fusion | flops 1769472 | bytes 21234528 | tf_op jit(solution)/shard_map/while/body/eval_jaxpr/scatter-add | solution.py:91
  353.7 5.7 fusion.91
  359.3 23.2 %scatter_fusion.1 = f32[16,64,128]{2,1,0:T(8,128)S(1)} fusion(f32[16,64,128]{2,1,0:T(8,128)S(1)} %bitcast.161, s32[216]{0:T(256)S(1)} %reshape.620, f32[216,64,128]{2,1,0:T(8,128)} %bitcast.168), kind=kCustom, calls=%fused_computation.3.clone.1 | custom fusion | flops 1769472 | bytes 21234528 | tf_op jit(solution)/shard_map/while/body/eval_jaxpr/scatter-add | solution.py:92
  388.3 7.1 %convolution_convert_fusion = bf16[1024,3072]{1,0:T(8,128)(2,1)} fusion(bf16[1024,384]{0,1:T(8,128)(2,1)S(1)} %bitcast.181, bf16[1,3072,1,384]{3,1,2,0:T(8,128)(2,1)} %param.13), kind=kOutput, calls=%fused_computation.48 | convolution fusion | flops 2419064832 | bytes 9437184 | tf_op jit(solution)/shard_map/tc,dc->td/dot_general | solution.py:199
  396.4 6.4 %fusion.44 = f32[1024,3072]{1,0:T(8,128)} fusion(bf16[1024,128]{1,0:T(8,128)(2,1)S(1)} %bitcast.184, bf16[1,128,3072]{2,1,0:T(8,128)(2,1)S(1)} %copy-done), kind=kOutput, calls=%fused_computation.59 | convolution fusion | flops 805306368 | bytes 13631488 | tf_op jit(solution)/shard_map/dot_general | solution.py:171
  402.7 58.6 %reduce-scatter.5.cloned.1.call-done = bf16[64,3072]{1,0:T(8,128)(2,1)} async-done(((bf16[1024,3072]{1,0:T(8,128)(2,1)}), bf16[64,3072]{1,0:T(8,128)(2,1)}) %reduce-scatter.5.cloned.1.call-update) | async-done | bytes 393232 | tf_op jit(solution)/shard_map/reduce_scatter | solution.py:198
  461.4 80.7 %reduce-scatter.3.cloned.1.call-done = f32[64,3072]{1,0:T(8,128)} async-done(((f32[1024,3072]{1,0:T(8,128)}), f32[64,3072]{1,0:T(8,128)}) %reduce-scatter.3.cloned.1.call-update) | async-done | bytes 786448 | tf_op jit(solution)/shard_map/reduce_scatter | solution.py:170
  548.1 46.7 %all-reduce = f32[3072]{0:T(1024)S(1)} all-reduce(f32[3072]{0:T(1024)S(1)} %get-tuple-element.116), channel_id=4, replica_groups=mesh['seq'=16,'pipe'=4,'dp'=4] {'seq'}, use_global_device_ids=true, to_apply=%region_17.18.clone | all-reduce | flops 3072 | bytes 24576
  (136 shorter events, 49.5 us)
Async XLA Ops:
  7.2 191.2 %copy-start = (bf16[1,128,3072]{2,1,0:T(8,128)(2,1)S(1)}, bf16[1,128,3072]{2,1,0:T(8,128)(2,1)}, u32[]{:S(2)}) copy-start(bf16[1,128,3072]{2,1,0:T(8,128)(2,1)} %param.14) | copy-start | bytes 2359300
  11.7 8.8 %copy-start.8 = (bf16[1,64,3072]{2,1,0:T(8,128)(2,1)S(1)}, bf16[1,64,3072]{2,1,0:T(8,128)(2,1)}, u32[]{:S(2)}) copy-start(bf16[1,64,3072]{2,1,0:T(8,128)(2,1)} %param.12) | copy-start | bytes 1179652
  11.7 8.8 %copy-start.17 = (f32[1,3072]{1,0:T(1,128)S(1)}, f32[1,3072]{1,0:T(1,128)}, u32[]{:S(2)}) copy-start(f32[1,3072]{1,0:T(1,128)} %param.17) | copy-start | bytes 36868
  11.7 177.5 %all-to-all-start = ((bf16[16,64,3072]{2,1,0:T(8,128)(2,1)}), bf16[16,64,3072]{2,1,0:T(8,128)(2,1)}, u32[]{:S(2)}, u32[]{:S(2)}) async-start(bf16[16,64,3072]{2,1,0:T(8,128)(2,1)} %stack.10), calls=%async_computation | async-start | bytes 12582912 | tf_op jit(solution)/shard_map/all_to_all | solution.py:131
  20.4 177.9 %all-gather.2.cloned.1.call-start = ((), (), s32[]{:S(2)}) async-start(), calls=%async_computation.3 | async-start | bytes 6684672 | tf_op jit(solution)/shard_map/all_gather | solution.py:152
  21.3 440.0 %reduce-scatter.5.cloned.1.call-start = ((), (), s32[]{:S(2)}) async-start(), calls=%async_computation.5 | async-start | bytes 6684672 | tf_op jit(solution)/shard_map/reduce_scatter | solution.py:198
  189.1 8.8 %copy-start.23 = (f32[1,128]{1,0:T(1,128)S(1)}, f32[1,128]{1,0:T(1,128)}, u32[]{:S(2)}) copy-start(f32[1,128]{1,0:T(1,128)} %param.15) | copy-start | bytes 1540
  189.1 9.0 %copy-start.25 = (f32[1,128]{1,0:T(1,128)S(1)}, f32[1,128]{1,0:T(1,128)}, u32[]{:S(2)}) copy-start(f32[1,128]{1,0:T(1,128)} %param.16) | copy-start | bytes 1540
  196.9 6.0 %copy-start.3 = (f32[1024,1,1,128]{3,0,2,1:T(8,128)}, f32[1024,1,1,128]{3,0,2,1:T(8,128)S(1)}, u32[]{:S(2)}) copy-start(f32[1024,1,1,128]{3,0,2,1:T(8,128)S(1)} %get-tuple-element.115) | copy-start | bytes 1572868
  196.9 6.0 %copy-start.5 = (f32[1024,1,1,128]{3,0,2,1:T(8,128)}, f32[1024,1,1,128]{3,0,2,1:T(8,128)S(1)}, u32[]{:S(2)}) copy-start(f32[1024,1,1,128]{3,0,2,1:T(8,128)S(1)} %get-tuple-element.114) | copy-start | bytes 1572868
  203.1 179.5 %copy-start.14 = (f32[16,64]{1,0:T(8,128)S(1)}, f32[16,64]{1,0:T(8,128)}, u32[]{:S(2)}) copy-start(f32[16,64]{1,0:T(8,128)} %copy-done.13) | copy-start | bytes 12292
  203.1 179.5 %copy-start.26 = (f32[1,128]{1,0:T(1,128)S(1)}, f32[1,128]{1,0:T(1,128)}, u32[]{:S(2)}) copy-start(f32[1,128]{1,0:T(1,128)} %param.16) | copy-start | bytes 1540
  203.1 180.9 %copy-start.4 = (f32[1024,1,1,128]{3,0,2,1:T(8,128)S(1)}, f32[1024,1,1,128]{3,0,2,1:T(8,128)}, u32[]{:S(2)}) copy-start(f32[1024,1,1,128]{3,0,2,1:T(8,128)} %copy-done.3) | copy-start | bytes 1572868
  203.2 180.9 %copy-start.21 = (f32[2,8,64]{2,1,0:T(8,128)S(1)}, f32[2,8,64]{2,1,0:T(8,128)}, u32[]{:S(2)}) copy-start(f32[2,8,64]{2,1,0:T(8,128)} %sqrt.32) | copy-start | bytes 12292
  203.2 180.9 %copy-start.24 = (f32[1,128]{1,0:T(1,128)S(1)}, f32[1,128]{1,0:T(1,128)}, u32[]{:S(2)}) copy-start(f32[1,128]{1,0:T(1,128)} %param.15) | copy-start | bytes 1540
  203.2 182.5 %copy-start.16 = (f32[1024]{0:T(1024)S(1)}, f32[1024]{0:T(1024)}, u32[]{:S(2)}) copy-start(f32[1024]{0:T(1024)} %copy-done.15) | copy-start | bytes 12292
  203.2 182.5 %copy-start.20 = (f32[1024]{0:T(1024)S(1)}, f32[1024]{0:T(1024)}, u32[]{:S(2)}) copy-start(f32[1024]{0:T(1024)} %copy-done.19) | copy-start | bytes 12292
  395.4 146.6 %reduce-scatter.3.cloned.1.call-start = ((), (), s32[]{:S(2)}) async-start(), calls=%async_computation.4 | async-start | bytes 13369344 | tf_op jit(solution)/shard_map/reduce_scatter | solution.py:170
  402.7 139.4 %copy-start.7 = (bf16[1,64,3072]{2,1,0:T(8,128)(2,1)S(1)}, bf16[1,64,3072]{2,1,0:T(8,128)(2,1)}, u32[]{:S(2)}) copy-start(bf16[1,64,3072]{2,1,0:T(8,128)(2,1)} %param.11) | copy-start | bytes 1179652
  402.7 139.4 %copy-start.9 = (bf16[1,64,3072]{2,1,0:T(8,128)(2,1)S(1)}, bf16[1,64,3072]{2,1,0:T(8,128)(2,1)}, u32[]{:S(2)}) copy-start(bf16[1,64,3072]{2,1,0:T(8,128)(2,1)} %param.12) | copy-start | bytes 1179652
  402.7 139.4 %copy-start.18 = (f32[1,3072]{1,0:T(1,128)S(1)}, f32[1,3072]{1,0:T(1,128)}, u32[]{:S(2)}) copy-start(f32[1,3072]{1,0:T(1,128)} %param.17) | copy-start | bytes 36868
  402.7 144.2 %copy-start.28 = (u32[256]{0:T(256)S(1)}, u32[256]{0:T(256)}, u32[]{:S(2)}) copy-start(u32[256]{0:T(256)} %constant.48) | copy-start | bytes 3076
  543.6 51.9 %collective-permute-start = (bf16[64,3072]{1,0:T(8,128)(2,1)S(1)}, bf16[64,3072]{1,0:T(8,128)(2,1)S(1)}, u32[]{:S(2)}, u32[]{:S(2)}) collective-permute-start(bf16[64,3072]{1,0:T(8,128)(2,1)S(1)} %get-tuple-element.117), channel_id=1, source_target_pairs={{12,0},{0,4},{4,8},{8,12},{13,1},{1,5},{5,9},{9,13},{14,2},{2,6},{... | collective-permute-start | bytes 1179656 | tf_op jit(solution)/shard_map/ppermute | solution.py:14
  545.1 50.4 %collective-permute-start.1 = (bf16[64,3072]{1,0:T(8,128)(2,1)S(1)}, bf16[64,3072]{1,0:T(8,128)(2,1)S(1)}, u32[]{:S(2)}, u32[]{:S(2)}) collective-permute-start(bf16[64,3072]{1,0:T(8,128)(2,1)S(1)} %get-tuple-element.118), channel_id=1, source_target_pairs={{4,0},{8,4},{12,8},{0,12},{5,1},{9,5},{13,9},{1,13},{6,2},{10,6},{... | collective-permute-start | bytes 1179656 | tf_op jit(solution)/shard_map/ppermute | solution.py:14
  (15 other events, 45.1 us)
Sparse Core Ops, SparseCore 0:
  23.7 133.6 all-gather.1
  395.6 65.7 reduce-scatter.4
  464.0 78.0 reduce-scatter.2
